TPU v7x, 32 devices: a whole 2x2x4 slice. The times are simulated.
32 devices in a mesh: dp: 4 (over y, x), seq: 8 (over z, core).
Axes of the slice: x: 2, y: 2, z: 4, core: 2. Of those that a mesh axis runs over, the one named last changes fastest.
Arguments:
- tiles: bfloat16 [4, 8192, 768], P('dp', 'seq'), may hold values from -48 to 48
- tile_count: int32 [4], P('dp'), may hold values from 4097 to 8192
- offsets: int32 [16], replicated, may hold values from 0 to 15
- w_query: bfloat16 [768, 768], replicated, may hold values from -0.375 to 0.375
- w_key: bfloat16 [768, 768], replicated, may hold values from -0.375 to 0.375
- w_value: bfloat16 [768, 768], replicated, may hold values from -0.21875 to 0.21875
- w_out: bfloat16 [768, 768], replicated, may hold values from -0.21875 to 0.21875
- cotangent: bfloat16 [4, 8192, 768], P('dp', 'seq'), may hold values from -0.046875 to 0.046875
Outputs:
- branch: bfloat16 [4, 8192, 768], P('dp', 'seq')
- grad_out: float32 [768, 768], P(None, 'seq')
All inputs are finite; a program needn't handle non-finite values.
Results may differ from a plain program's by a relative error of at most 0.0095.
The roundings to bfloat16 on the way count: a program that leaves them out, or rounds other values in their place, can miss the bound.
Values may be sent and summed in bfloat16 or wider, within the bound.
A program may use at most 128 MiB of HBM per device.

v0:
```python
import jax
import jax.numpy as jnp
from jax import lax
from jax.sharding import PartitionSpec as P

D = 768
ATTENTION_HEADS = 16
HEAD_SIZE = 48
SEG = 1024
RATE = 16
NEGATIVE_FLOOR = -1e30
head_group = 4


def project(inputs, weight):
    return jnp.dot(inputs, weight, preferred_element_type=jnp.float32).astype(jnp.bfloat16)


def select_rows(tensor, offsets):
    segment_height = tensor.shape[0]
    grouped = tensor.reshape(segment_height // RATE, RATE, ATTENTION_HEADS, HEAD_SIZE)
    onehot = (jnp.arange(RATE, dtype=jnp.int32)[:, None] == offsets[None, :]).astype(jnp.bfloat16)
    return jnp.einsum("arhd,rh->ahd", grouped, onehot, preferred_element_type=jnp.float32).astype(
        jnp.bfloat16
    )


def local_attention(query_proj, key_proj, value_proj, is_live):
    segment_height = query_proj.shape[0]
    segments = segment_height // SEG
    groups = ATTENTION_HEADS // head_group
    query_seg = query_proj.reshape(segments, SEG, groups, head_group, HEAD_SIZE)
    key_seg = key_proj.reshape(segments, SEG, groups, head_group, HEAD_SIZE)
    value_seg = value_proj.reshape(segments, SEG, groups, head_group, HEAD_SIZE)
    alive_seg = is_live.reshape(segments, SEG)

    def one_group(index):
        query_part = lax.dynamic_index_in_dim(query_seg, index, 2, keepdims=False)
        key_part = lax.dynamic_index_in_dim(key_seg, index, 2, keepdims=False)
        value_part = lax.dynamic_index_in_dim(value_seg, index, 2, keepdims=False)
        scores = jnp.einsum(
            "sqhd,skhd->shqk", query_part, key_part, preferred_element_type=jnp.float32
        ) * HEAD_SIZE ** (-0.5)
        scores = jnp.where(alive_seg[:, None, None, :], scores, NEGATIVE_FLOOR)
        maxima = jnp.max(scores, axis=-1)
        weights = jnp.exp(scores - maxima[..., None])
        totals = jnp.sum(weights, axis=-1)
        weighted = jnp.einsum(
            "shqk,skhd->sqhd",
            weights.astype(jnp.bfloat16),
            value_part,
            preferred_element_type=jnp.float32,
        )
        return (maxima, totals, weighted)

    maxima, totals, weighted = lax.map(one_group, jnp.arange(groups, dtype=jnp.int32))
    maxima = maxima.transpose(1, 3, 0, 2).reshape(segment_height, ATTENTION_HEADS)
    totals = totals.transpose(1, 3, 0, 2).reshape(segment_height, ATTENTION_HEADS)
    weighted = weighted.transpose(1, 2, 0, 3, 4).reshape(segment_height, ATTENTION_HEADS, HEAD_SIZE)
    return (maxima, totals, weighted)


def combine(local, dilated_branch, offsets, is_live):
    local_max, local_total, local_sum = local
    dilated_row_max, dilated_value_total, dilated_row_sum = dilated_branch
    segment_height = local_max.shape[0]
    dilation_match = jnp.arange(RATE, dtype=jnp.int32)[:, None] == offsets[None, :]
    dense_row_max = jnp.where(
        dilation_match[None], dilated_row_max[:, None, :], NEGATIVE_FLOOR
    ).reshape(segment_height, ATTENTION_HEADS)
    dense_value_total = jnp.where(
        dilation_match[None], dilated_value_total[:, None, :], 0.0
    ).reshape(segment_height, ATTENTION_HEADS)
    dense_row_sum = jnp.where(
        dilation_match[None, :, :, None], dilated_row_sum[:, None], 0.0
    ).reshape(segment_height, ATTENTION_HEADS, HEAD_SIZE)
    top = jnp.maximum(local_max, dense_row_max)
    near = jnp.exp(local_max - top)
    far = jnp.exp(dense_row_max - top)
    attn = (near[..., None] * local_sum + far[..., None] * dense_row_sum) / (
        near * local_total + far * dense_value_total
    )[..., None]
    attn = jnp.where(is_live[:, None, None], attn, 0.0)
    return attn.reshape(segment_height, D).astype(jnp.bfloat16)


def body(tiles, tile_count, offsets, w_query, w_key, w_value, w_out, cotangent):
    inputs = tiles[0]
    segment_height = inputs.shape[0]
    shard_rank = lax.axis_index("seq")
    live_count = tile_count[0]
    query_proj = project(inputs, w_query).reshape(segment_height, ATTENTION_HEADS, HEAD_SIZE)
    key_proj = project(inputs, w_key).reshape(segment_height, ATTENTION_HEADS, HEAD_SIZE)
    value_proj = project(inputs, w_value).reshape(segment_height, ATTENTION_HEADS, HEAD_SIZE)
    positions = shard_rank * segment_height + jnp.arange(segment_height, dtype=jnp.int32)
    is_live = positions < live_count
    local = local_attention(query_proj, key_proj, value_proj, is_live)
    picked = segment_height // RATE
    query_sel = select_rows(query_proj, offsets)
    key_sel = select_rows(key_proj, offsets)
    value_sel = select_rows(value_proj, offsets)
    score_scale = HEAD_SIZE ** (-0.5)
    portion = (
        lax.all_gather(key_sel.reshape(picked, D), "seq", axis=0, tiled=True),
        lax.all_gather(value_sel.reshape(picked, D), "seq", axis=0, tiled=True),
    )
    old_max = jnp.full((picked, ATTENTION_HEADS), NEGATIVE_FLOOR, jnp.float32)
    key_part = portion[0].reshape(portion[0].shape[0], ATTENTION_HEADS, HEAD_SIZE)
    value_part = portion[1].reshape(portion[1].shape[0], ATTENTION_HEADS, HEAD_SIZE)
    amount = key_part.shape[0]
    key_live = jnp.arange(amount, dtype=jnp.int32)[:, None] * RATE + offsets[None, :] < live_count
    scores = (
        jnp.einsum("qhd,khd->qhk", query_sel, key_part, preferred_element_type=jnp.float32)
        * score_scale
    )
    scores = jnp.where(key_live.T[None], scores, NEGATIVE_FLOOR)
    new_max = jnp.maximum(old_max, jnp.max(scores, axis=-1))
    weights = jnp.exp(scores - new_max[..., None])
    new_total = jnp.sum(weights, axis=-1)
    new_sum = jnp.einsum(
        "qhk,khd->qhd", weights.astype(jnp.bfloat16), value_part, preferred_element_type=jnp.float32
    )
    dilated_branch = (new_max, new_total, new_sum)
    attn = combine(local, dilated_branch, offsets, is_live)
    branch = jnp.dot(attn, w_out, preferred_element_type=jnp.float32).astype(jnp.bfloat16)[None]
    gradient_in = cotangent[0]
    shares = lax.psum_scatter(
        jnp.einsum("tc,td->cd", gradient_in, attn, preferred_element_type=jnp.float32),
        "seq",
        scatter_dimension=0,
        tiled=True,
    )
    grad_part = lax.psum(shares.astype(jnp.bfloat16), "dp").astype(jnp.float32).T
    return (branch, grad_part)


def solution(mesh):
    in_specs = (P("dp", "seq", None), P("dp"), P(), P(), P(), P(), P(), P("dp", "seq", None))
    out_specs = (P("dp", "seq", None), P(None, "seq"))
    return jax.shard_map(body, mesh=mesh, in_specs=in_specs, out_specs=out_specs, check_vma=False)
```

profile of v0, /device:TPU:0, one launch (start us, length us, event | category | flops | bytes accessed | tf_op | source)
XLA Modules:
  0.0 290.6 jit_solution(8163011718679875207)
XLA Ops:
  23.6 7.2 %reshape_reshape.22 = bf16[64,16,16,48]{3,2,1,0:T(8,128)(2,1)} reshape(bf16[1024,768]{1,0:T(8,128)(2,1)} %copy.47) | data formatting | bytes 3145728 | tf_op jit(solution)/shard_map/reshape;reshape | solution.py:21
  30.8 7.2 %reshape_reshape.21 = bf16[64,16,16,48]{3,2,1,0:T(8,128)(2,1)} reshape(bf16[1024,768]{1,0:T(8,128)(2,1)} %copy.45) | data formatting | bytes 3145728 | tf_op jit(solution)/shard_map/reshape;reshape | solution.py:21
  38.0 7.2 %reshape_reshape.23 = bf16[64,16,16,48]{3,2,1,0:T(8,128)(2,1)} reshape(bf16[1024,768]{1,0:T(8,128)(2,1)} %copy.49) | data formatting | bytes 3145728 | tf_op jit(solution)/shard_map/reshape;reshape | solution.py:21
  45.2 9.0 %multiply_reduce_fusion.1 = (bf16[16,64,48]{2,0,1:T(8,128)(2,1)S(1)}, bf16[16,64,48]{2,0,1:T(8,128)(2,1)}, bf16[16,64,48]{2,0,1:T(8,128)(2,1)}) fusion(f32[16,16]{0,1:T(8,128)S(1)} %copy.80, bf16[64,16,16,48]{3,2,1,0:T(8,128)(2,1)} %reshape_reshape.22, bf16[64,16,16,48]{3,2,1,0:T(8,128)(2,1)} %reshape_reshape.23, bf16[64,16,16,48]{3,2,1,0:T(8,128)(2,1)} %reshape_reshape.21), kind=kLoop, calls=%fused_computation.25 | loop fusion | flops 6930432 | bytes 5014528
  57.5 18.4 %all_gather.6 = bf16[512,768]{1,0:T(8,128)(2,1)} all-gather(bf16[64,768]{1,0:T(8,128)(2,1)S(1)} %reshape.263), channel_id=1, replica_groups=mesh['dp'=4,'seq'=8] {'seq'}, dimensions={0}, use_global_device_ids=true | all-gather | bytes 884736 | tf_op jit(solution)/shard_map/all_gather | solution.py:104
  78.3 16.6 %all_gather.7 = bf16[512,768]{1,0:T(8,128)(2,1)} all-gather(bf16[64,768]{1,0:T(8,128)(2,1)S(1)} %reshape.266), channel_id=1, replica_groups=mesh['dp'=4,'seq'=8] {'seq'}, dimensions={0}, use_global_device_ids=true | all-gather | bytes 884736 | tf_op jit(solution)/shard_map/all_gather | solution.py:105
  108.7 66.5 %while.15 = (s32[]{:T(128)}, f32[4,1,4,1024]{3,2,1,0:T(4,128)}, f32[4,1,4,1024]{3,2,1,0:T(4,128)}, f32[4,1,1024,4,48]{2,4,3,1,0:T(8,128)}, s32[4]{0:T(128)S(1)},...) while((s32[]{:T(128)}, f32[4,1,4,1024]{3,2,1,0:T(4,128)}, ...), condition=%wide.region_3.4_spmd.clone, body=%wide.region_0.3_spmd.clone.sunk | while | flops 851437568 | bytes 52434116 | solution.py:56
  115.0 4.1 %fusion.71 = f32[4,1024]{1,0:T(4,128)S(1)} fusion(f32[4,1024,1024]{1,2,0:T(8,128)S(1)} %get-tuple-element.187, f32[4,1024]{1,0:T(4,128)S(1)} %get-tuple-element.188, pred[1024]{0:T(1024)(128)(4,1)S(1)} %add_compare_fusion.4), kind=kLoop, calls=%fused_computation.5.clone.1 | loop fusion | flops 16773120 | bytes 16811008 | tf_op jit(solution)/shard_map/while/body/eval_jaxpr/reduce_sum | solution.py:47
  119.1 5.7 %fusion.72 = f32[4,1,1024,4,48]{2,4,3,1,0:T(8,128)} fusion(f32[4,1,1024,4,48]{2,4,3,1,0:T(8,128)} %get-tuple-element.207, s32[]{:T(128)S(6)} %copy.89, f32[4,1024,1024]{1,2,0:T(8,128)S(1)} %get-tuple-element.187, f32[4,1024]{1,0:T(4,128)S(1)} %get-tuple-element.188, pred[1024]{0:T(1024)(128)(4,1)S(1)} %add_compare_fusion.4, ...), kind=kOutput, calls=%fused_computation.9.clone.1 | convolution fusion | flops 419430400 | bytes 17974280 | tf_op jit(solution)/shard_map/while/body/eval_jaxpr/shqk,skhd->sqhd/dot_general | solution.py:48
  131.6 4.1 %fusion.71 = f32[4,1024]{1,0:T(4,128)S(1)} fusion(f32[4,1024,1024]{1,2,0:T(8,128)S(1)} %get-tuple-element.187, f32[4,1024]{1,0:T(4,128)S(1)} %get-tuple-element.188, pred[1024]{0:T(1024)(128)(4,1)S(1)} %add_compare_fusion.4), kind=kLoop, calls=%fused_computation.5.clone.1 | loop fusion | flops 16773120 | bytes 16811008 | tf_op jit(solution)/shard_map/while/body/eval_jaxpr/reduce_sum | solution.py:47
  135.8 5.6 %fusion.72 = f32[4,1,1024,4,48]{2,4,3,1,0:T(8,128)} fusion(f32[4,1,1024,4,48]{2,4,3,1,0:T(8,128)} %get-tuple-element.207, s32[]{:T(128)S(6)} %copy.89, f32[4,1024,1024]{1,2,0:T(8,128)S(1)} %get-tuple-element.187, f32[4,1024]{1,0:T(4,128)S(1)} %get-tuple-element.188, pred[1024]{0:T(1024)(128)(4,1)S(1)} %add_compare_fusion.4, ...), kind=kOutput, calls=%fused_computation.9.clone.1 | convolution fusion | flops 419430400 | bytes 17974280 | tf_op jit(solution)/shard_map/while/body/eval_jaxpr/shqk,skhd->sqhd/dot_general | solution.py:48
  148.3 4.1 %fusion.71 = f32[4,1024]{1,0:T(4,128)S(1)} fusion(f32[4,1024,1024]{1,2,0:T(8,128)S(1)} %get-tuple-element.187, f32[4,1024]{1,0:T(4,128)S(1)} %get-tuple-element.188, pred[1024]{0:T(1024)(128)(4,1)S(1)} %add_compare_fusion.4), kind=kLoop, calls=%fused_computation.5.clone.1 | loop fusion | flops 16773120 | bytes 16811008 | tf_op jit(solution)/shard_map/while/body/eval_jaxpr/reduce_sum | solution.py:47
  152.4 5.6 %fusion.72 = f32[4,1,1024,4,48]{2,4,3,1,0:T(8,128)} fusion(f32[4,1,1024,4,48]{2,4,3,1,0:T(8,128)} %get-tuple-element.207, s32[]{:T(128)S(6)} %copy.89, f32[4,1024,1024]{1,2,0:T(8,128)S(1)} %get-tuple-element.187, f32[4,1024]{1,0:T(4,128)S(1)} %get-tuple-element.188, pred[1024]{0:T(1024)(128)(4,1)S(1)} %add_compare_fusion.4, ...), kind=kOutput, calls=%fused_computation.9.clone.1 | convolution fusion | flops 419430400 | bytes 17974280 | tf_op jit(solution)/shard_map/while/body/eval_jaxpr/shqk,skhd->sqhd/dot_general | solution.py:48
  164.9 4.1 %fusion.71 = f32[4,1024]{1,0:T(4,128)S(1)} fusion(f32[4,1024,1024]{1,2,0:T(8,128)S(1)} %get-tuple-element.187, f32[4,1024]{1,0:T(4,128)S(1)} %get-tuple-element.188, pred[1024]{0:T(1024)(128)(4,1)S(1)} %add_compare_fusion.4), kind=kLoop, calls=%fused_computation.5.clone.1 | loop fusion | flops 16773120 | bytes 16811008 | tf_op jit(solution)/shard_map/while/body/eval_jaxpr/reduce_sum | solution.py:47
  169.0 5.6 %fusion.72 = f32[4,1,1024,4,48]{2,4,3,1,0:T(8,128)} fusion(f32[4,1,1024,4,48]{2,4,3,1,0:T(8,128)} %get-tuple-element.207, s32[]{:T(128)S(6)} %copy.89, f32[4,1024,1024]{1,2,0:T(8,128)S(1)} %get-tuple-element.187, f32[4,1024]{1,0:T(4,128)S(1)} %get-tuple-element.188, pred[1024]{0:T(1024)(128)(4,1)S(1)} %add_compare_fusion.4, ...), kind=kOutput, calls=%fused_computation.9.clone.1 | convolution fusion | flops 419430400 | bytes 17974280 | tf_op jit(solution)/shard_map/while/body/eval_jaxpr/shqk,skhd->sqhd/dot_general | solution.py:48
  176.9 4.9 %broadcast_in_dim.156 = f32[64,16,16,48]{3,2,1,0:T(8,128)} broadcast(f32[64,16,48]{2,1,0:T(8,128)} %copy.51), dimensions={0,2,3} | broadcast | bytes 3342336 | tf_op jit(solution)/shard_map/jit(_where)/broadcast_in_dim | solution.py:74
  181.9 6.6 %copy.53 = f32[1024,16,48]{0,2,1:T(8,128)} copy(f32[1024,16,48]{2,1,0:T(8,128)} %bitcast.162) | data formatting | bytes 6291456 | tf_op jit(solution)/shard_map/jit(_where)/broadcast_in_dim | solution.py:74
  188.5 4.0 %fusion.32 = bf16[1024,16,48]{0,2,1:T(8,128)(2,1)S(1)} fusion(f32[1024,16,48]{0,2,1:T(8,128)} %copy.53, f32[4,1,1024,4,48]{2,4,3,1,0:T(8,128)} %get-tuple-element.52, f32[1024,16]{0,1:T(8,128)S(1)} %get-tuple-element.111, f32[1024,16]{0,1:T(8,128)S(1)} %get-tuple-element.113, f32[1024,16]{0,1:T(8,128)S(1)} %get-tuple-element.112, ...), kind=kLoop, calls=%fused_computation.37 | loop fusion | flops 5505024 | bytes 8078336 | tf_op jit(solution)/shard_map/convert_element_type | solution.py:84
  198.5 7.9 %broadcast_in_dim.157 = f32[1024,768]{1,0:T(8,128)} reshape(f32[64,16,16,48]{3,2,1,0:T(8,128)} %broadcast_in_dim.156) | data formatting | bytes 6291456 | tf_op jit(solution)/shard_map/jit(_where)/broadcast_in_dim | solution.py:74
  206.5 3.6 %copy.52 = f32[1024,768]{0,1:T(8,128)} copy(f32[1024,768]{1,0:T(8,128)} %broadcast_in_dim.157) | data formatting | bytes 6291456 | tf_op jit(solution)/shard_map/jit(_where)/broadcast_in_dim | solution.py:74
  210.0 3.9 %fusion.31 = bf16[1024,768]{0,1:T(8,128)(2,1)S(1)} fusion(f32[1024,768]{0,1:T(8,128)} %copy.52, f32[4,1,1024,4,48]{2,4,3,1,0:T(8,128)} %get-tuple-element.52, f32[1024,16]{0,1:T(8,128)S(1)} %get-tuple-element.111, f32[1024,16]{0,1:T(8,128)S(1)} %get-tuple-element.113, f32[1024,16]{0,1:T(8,128)S(1)} %get-tuple-element.112, ...), kind=kLoop, calls=%fused_computation.36 | loop fusion | flops 5505024 | bytes 8078336 | tf_op jit(solution)/shard_map/convert_element_type | solution.py:84
  213.9 23.1 %reduce-scatter.4.cloned.1.call-done = f32[96,768]{1,0:T(8,128)} async-done(((f32[768,768]{1,0:T(8,128)}), f32[96,768]{1,0:T(8,128)}) %reduce-scatter.4.cloned.1.call-update) | async-done | bytes 294928
  238.8 4.0 %fusion.40 = bf16[1,1024,768]{2,1,0:T(8,128)(2,1)} fusion(bf16[1024,768]{0,1:T(8,128)(2,1)S(1)} %fusion.31, bf16[768,768]{1,0:T(8,128)(2,1)} %param.16), kind=kOutput, calls=%fused_computation.53 | convolution fusion | flops 1208745984 | bytes 4325376 | tf_op jit(solution)/shard_map/dot_general | solution.py:125
  242.7 39.3 %all-reduce.2.cloned.1.call-done = bf16[768,96]{1,0:T(8,128)(2,1)} async-done(((bf16[768,96]{1,0:T(8,128)(2,1)}), bf16[768,96]{1,0:T(8,128)(2,1)}) %all-reduce.2.cloned.1.call-update) | async-done | bytes 147472 | tf_op jit(solution)/shard_map/psum | solution.py:133
  (84 shorter events, 67.3 us)
Async XLA Ops:
  7.2 2.5 copy-start
  7.2 229.8 %reduce-scatter.4.cloned.1.call-start = ((), (), s32[]{:S(2)}) async-start(), calls=%async_computation.2 | async-start | bytes 2654208
  9.6 2.8 copy-start.11
  12.5 2.6 copy-start.12
  17.7 2.8 copy-start.2
  57.5 39.7 %copy-start.3 = (bf16[16,64,48]{1,2,0:T(8,128)(2,1)S(1)}, bf16[16,64,48]{1,2,0:T(8,128)(2,1)}, u32[]{:S(2)}) copy-start(bf16[16,64,48]{1,2,0:T(8,128)(2,1)} %copy.70) | copy-start | bytes 294916
  76.0 21.2 %copy-start.8 = (s32[512]{0:T(512)S(1)}, s32[512]{0:T(512)}, u32[]{:S(2)}) copy-start(s32[512]{0:T(512)} %iota_multiply_fusion) | copy-start | bytes 6148
  76.0 21.2 %copy-start.9 = (s32[16]{0:T(128)S(1)}, s32[16]{0:T(128)}, u32[]{:S(2)}) copy-start(s32[16]{0:T(128)} %param.12) | copy-start | bytes 196
  97.2 3.2 %copy-start.4 = (bf16[512,768]{0,1:T(8,128)(2,1)S(1)}, bf16[512,768]{0,1:T(8,128)(2,1)}, u32[]{:S(2)}) copy-start(bf16[512,768]{0,1:T(8,128)(2,1)} %copy.50) | copy-start | bytes 2359300
  99.1 1.4 copy-start.5
  181.9 6.6 %copy-start.6 = (pred[1024]{0:T(1024)(128)(4,1)S(1)}, pred[1024]{0:T(1024)(128)(4,1)}, u32[]{:S(2)}) copy-start(pred[1024]{0:T(1024)(128)(4,1)} %add_compare_fusion.2) | copy-start | bytes 3076
  188.5 4.0 %copy-start.10 = (bf16[1,1024,768]{2,1,0:T(8,128)(2,1)S(1)}, bf16[1,1024,768]{2,1,0:T(8,128)(2,1)}, u32[]{:S(2)}) copy-start(bf16[1,1024,768]{2,1,0:T(8,128)(2,1)} %param.17) | copy-start | bytes 4718596
  198.5 83.5 %all-reduce.2.cloned.1.call-start = ((), (), s32[]{:S(2)}) async-start(), calls=%async_computation.1 | async-start | bytes 393216 | tf_op jit(solution)/shard_map/psum | solution.py:133
  206.5 3.6 %copy-start.7 = (pred[1024]{0:T(1024)(128)(4,1)S(1)}, pred[1024]{0:T(1024)(128)(4,1)}, u32[]{:S(2)}) copy-start(pred[1024]{0:T(1024)(128)(4,1)} %add_compare_fusion.2) | copy-start | bytes 3076
  238.7 45.0 %copy-start.1 = (bf16[1,1024,768]{2,1,0:T(8,128)(2,1)S(1)}, bf16[1,1024,768]{2,1,0:T(8,128)(2,1)}, u32[]{:S(2)}) copy-start(bf16[1,1024,768]{2,1,0:T(8,128)(2,1)} %param.10) | copy-start | bytes 4718596
Sparse Core Ops, SparseCore 0:
  198.6 38.3 reduce-scatter.3
  240.4 41.5 all-reduce.1
where the time goes:
time: 292 us; the launch traced here: 291 us
  local copies, waits for them, and re-layouts  79 us (27%)
  waiting for transfers between devices  62.4 us (21%)
  matrix products  53.2 us (18%)
  other arithmetic  39.2 us (13%)
  blocking collectives  35 us (12%)
  between operations  14.9 us (5%)
  loops' own time  6.89 us (2%)
    psum x1, waiting for transfers between devices, body(): lax.psum(shares.astype(jnp.bfloat16), 'dp').astype(jnp.float32)  39.3 us
    unnamed x3, waiting for transfers between devices  23.1 us
    broadcast_in_dim x4, local copies, waits for them, and re-layouts, combine(): jnp.where(dilation_match[None, :, :, None], dilated_row_sum[:, None], 0.0)  23 us
    dot_general x4, matrix products, one_group(): jnp.einsum('shqk,skhd->sqhd', weights.astype(jnp.bfloat16), value_part, p...  22.5 us
    another operation x3, local copies, waits for them, and re-layouts, select_rows(): tensor.reshape(segment_height // RATE, RATE, ATTENTION_HEADS, HEAD_SIZE)  21.5 us
    all_gather x1, blocking collectives, body(): lax.all_gather(key_sel.reshape(picked, D), 'seq', axis=0, tiled=True)  18.4 us
    all_gather x1, blocking collectives, body(): lax.all_gather(value_sel.reshape(picked, D), 'seq', axis=0, tiled=True)  16.6 us
    reduce_sum x4, other arithmetic, one_group(): totals = jnp.sum(weights, axis=-1)  16.4 us
  transfers between devices with their start and end apart: 2, of which 2 were waited for; matrix products, arithmetic and copies ran while one was open for 7% of the time, Pallas kernels for 0%

commit v1 on v0

--- a/solution.py
+++ b/solution.py
@@ -100,8 +100,12 @@
     key_sel = select_rows(key_proj, offsets)
     value_sel = select_rows(value_proj, offsets)
     score_scale = HEAD_SIZE ** (-0.5)
+    groups_plan = lambda raw, axis_key: jnp.concatenate(
+        jax.lax.all_to_all(jnp.stack([raw] * jax.lax.axis_size(axis_key), 0), axis_key, 0, 0),
+        axis=0,
+    )
     portion = (
-        lax.all_gather(key_sel.reshape(picked, D), "seq", axis=0, tiled=True),
+        groups_plan(key_sel.reshape(picked, D), "seq"),
         lax.all_gather(value_sel.reshape(picked, D), "seq", axis=0, tiled=True),
     )
     old_max = jnp.full((picked, ATTENTION_HEADS), NEGATIVE_FLOOR, jnp.float32)

time: 292 us -> 268 us (0.918)
  blocking collectives: 35 us -> 16.1 us
  local copies, waits for them, and re-layouts: 79 us -> 69.1 us
  starting transfers between devices: 0.08 us -> 6.69 us
    all_gather x1 -> x0, blocking collectives: 18.4 us -> none  [body(): lax.all_gather(key_sel.reshape(picked, D), 'seq', axis=0, tiled=True)]
    all_to_all x0 -> x1, starting transfers between devices: none -> 6.35 us  [body(): jax.lax.all_to_all(jnp.stack([raw] * jax.lax.axis_size(axis_key), 0), axi...]
    another operation x0 -> x3, local copies, waits for them, and re-layouts: none -> 3.12 us  [the longest x2 2.16 us: body(): jnp.stack([raw] * jax.lax.axis_size(axis_key), 0)]
    unnamed x30 -> x26, local copies, waits for them, and re-layouts: 6.73 us -> 6.71 us
  transfers between devices with their start and end apart: 2 -> 3, of which waited for: 2 -> 2; matrix products, arithmetic and copies ran while one was open for 7% -> 31% of each run, Pallas kernels for 0% -> 0%
where the time goes in v1:
time: 268 us; the launch traced here: 267 us
  local copies, waits for them, and re-layouts  69.1 us (26%)
  waiting for transfers between devices  62.6 us (23%)
  matrix products  52.1 us (19%)
  other arithmetic  38.7 us (14%)
  blocking collectives  16.1 us (6%)
  between operations  15 us (6%)
  loops' own time  6.92 us (3%)
  starting transfers between devices  6.69 us (2%)
    psum x1, waiting for transfers between devices, body(): lax.psum(shares.astype(jnp.bfloat16), 'dp').astype(jnp.float32)  39.2 us
    unnamed x3, waiting for transfers between devices  23.4 us
    dot_general x4, matrix products, one_group(): jnp.einsum('shqk,skhd->sqhd', weights.astype(jnp.bfloat16), value_part, p...  22.6 us
    broadcast_in_dim x4, local copies, waits for them, and re-layouts, combine(): jnp.where(dilation_match[None, :, :, None], dilated_row_sum[:, None], 0.0)  21.7 us
    another operation x3, local copies, waits for them, and re-layouts, select_rows(): tensor.reshape(segment_height // RATE, RATE, ATTENTION_HEADS, HEAD_SIZE)  21.5 us
    reduce_sum x4, other arithmetic, one_group(): totals = jnp.sum(weights, axis=-1)  16.4 us
    all_gather x1, blocking collectives, body(): lax.all_gather(value_sel.reshape(picked, D), 'seq', axis=0, tiled=True)  16.1 us
    dot_general x4, matrix products, one_group(): jnp.einsum('sqhd,skhd->shqk', query_part, key_part, preferred_element_typ...  13.4 us
  transfers between devices with their start and end apart: 3, of which 2 were waited for; matrix products, arithmetic and copies ran while one was open for 31% of the time, Pallas kernels for 0%

profile of v1, /device:TPU:0, one launch (start us, length us, event | category | flops | bytes accessed | tf_op | source)
XLA Modules:
  0.0 267.2 jit_solution(2130367453017860000)
XLA Ops:
  22.6 7.2 %reshape_reshape.26 = bf16[64,16,16,48]{3,2,1,0:T(8,128)(2,1)} reshape(bf16[1024,768]{1,0:T(8,128)(2,1)} %copy.47) | data formatting | bytes 3145728 | tf_op jit(solution)/shard_map/reshape;reshape | solution.py:21
  29.8 7.2 %reshape_reshape.24 = bf16[64,16,16,48]{3,2,1,0:T(8,128)(2,1)} reshape(bf16[1024,768]{1,0:T(8,128)(2,1)} %copy.45) | data formatting | bytes 3145728 | tf_op jit(solution)/shard_map/reshape;reshape | solution.py:21
  37.0 7.2 %reshape_reshape.27 = bf16[64,16,16,48]{3,2,1,0:T(8,128)(2,1)} reshape(bf16[1024,768]{1,0:T(8,128)(2,1)} %copy.49) | data formatting | bytes 3145728 | tf_op jit(solution)/shard_map/reshape;reshape | solution.py:21
  44.1 9.0 %multiply_reduce_fusion.1 = (bf16[16,64,48]{2,0,1:T(8,128)(2,1)S(1)}, bf16[16,64,48]{2,0,1:T(8,128)(2,1)}, bf16[16,64,48]{2,0,1:T(8,128)(2,1)}) fusion(f32[16,16]{0,1:T(8,128)S(1)} %copy.80, bf16[64,16,16,48]{3,2,1,0:T(8,128)(2,1)} %reshape_reshape.26, bf16[64,16,16,48]{3,2,1,0:T(8,128)(2,1)} %reshape_reshape.27, bf16[64,16,16,48]{3,2,1,0:T(8,128)(2,1)} %reshape_reshape.24), kind=kLoop, calls=%fused_computation.25 | loop fusion | flops 6930432 | bytes 5014528
  55.3 6.4 %all-to-all-start = ((bf16[8,64,768]{2,1,0:T(8,128)(2,1)}), bf16[8,64,768]{2,1,0:T(8,128)(2,1)}, u32[]{:S(2)}, u32[]{:S(2)}) async-start(bf16[8,64,768]{2,1,0:T(8,128)(2,1)} %stack.3), calls=%async_computation | async-start | bytes 1572864 | tf_op jit(solution)/shard_map/all_to_all | solution.py:104
  61.7 66.5 %while.15 = (s32[]{:T(128)}, f32[4,1,4,1024]{3,2,1,0:T(4,128)S(1)}, f32[4,1,4,1024]{3,2,1,0:T(4,128)}, f32[4,1,1024,4,48]{2,4,3,1,0:T(8,128)}, s32[4]{0:T(128)S(...) while((s32[]{:T(128)}, f32[4,1,4,1024]{3,2,1,0:T(4,128)S(1)}, ...), condition=%wide.region_3.4_spmd.clone, body=%wide.region_0.3_spmd.clone.sunk | while | flops 851437568 | bytes 52434116 | solution.py:56
  68.0 4.1 %fusion.71 = f32[4,1024]{1,0:T(4,128)S(1)} fusion(f32[4,1024,1024]{1,2,0:T(8,128)S(1)} %get-tuple-element.187, f32[4,1024]{1,0:T(4,128)S(1)} %get-tuple-element.188, pred[1024]{0:T(1024)(128)(4,1)S(1)} %add_compare_fusion.4), kind=kLoop, calls=%fused_computation.5.clone.1 | loop fusion | flops 16773120 | bytes 16811008 | tf_op jit(solution)/shard_map/while/body/eval_jaxpr/reduce_sum | solution.py:47
  72.1 5.7 %fusion.72 = f32[4,1,1024,4,48]{2,4,3,1,0:T(8,128)} fusion(f32[4,1,1024,4,48]{2,4,3,1,0:T(8,128)} %get-tuple-element.207, s32[]{:T(128)S(6)} %copy.89, f32[4,1024,1024]{1,2,0:T(8,128)S(1)} %get-tuple-element.187, f32[4,1024]{1,0:T(4,128)S(1)} %get-tuple-element.188, pred[1024]{0:T(1024)(128)(4,1)S(1)} %add_compare_fusion.4, ...), kind=kOutput, calls=%fused_computation.9.clone.1 | convolution fusion | flops 419430400 | bytes 17974280 | tf_op jit(solution)/shard_map/while/body/eval_jaxpr/shqk,skhd->sqhd/dot_general | solution.py:48
  84.7 4.1 %fusion.71 = f32[4,1024]{1,0:T(4,128)S(1)} fusion(f32[4,1024,1024]{1,2,0:T(8,128)S(1)} %get-tuple-element.187, f32[4,1024]{1,0:T(4,128)S(1)} %get-tuple-element.188, pred[1024]{0:T(1024)(128)(4,1)S(1)} %add_compare_fusion.4), kind=kLoop, calls=%fused_computation.5.clone.1 | loop fusion | flops 16773120 | bytes 16811008 | tf_op jit(solution)/shard_map/while/body/eval_jaxpr/reduce_sum | solution.py:47
  88.8 5.6 %fusion.72 = f32[4,1,1024,4,48]{2,4,3,1,0:T(8,128)} fusion(f32[4,1,1024,4,48]{2,4,3,1,0:T(8,128)} %get-tuple-element.207, s32[]{:T(128)S(6)} %copy.89, f32[4,1024,1024]{1,2,0:T(8,128)S(1)} %get-tuple-element.187, f32[4,1024]{1,0:T(4,128)S(1)} %get-tuple-element.188, pred[1024]{0:T(1024)(128)(4,1)S(1)} %add_compare_fusion.4, ...), kind=kOutput, calls=%fused_computation.9.clone.1 | convolution fusion | flops 419430400 | bytes 17974280 | tf_op jit(solution)/shard_map/while/body/eval_jaxpr/shqk,skhd->sqhd/dot_general | solution.py:48
  101.3 4.1 %fusion.71 = f32[4,1024]{1,0:T(4,128)S(1)} fusion(f32[4,1024,1024]{1,2,0:T(8,128)S(1)} %get-tuple-element.187, f32[4,1024]{1,0:T(4,128)S(1)} %get-tuple-element.188, pred[1024]{0:T(1024)(128)(4,1)S(1)} %add_compare_fusion.4), kind=kLoop, calls=%fused_computation.5.clone.1 | loop fusion | flops 16773120 | bytes 16811008 | tf_op jit(solution)/shard_map/while/body/eval_jaxpr/reduce_sum | solution.py:47
  105.4 5.6 %fusion.72 = f32[4,1,1024,4,48]{2,4,3,1,0:T(8,128)} fusion(f32[4,1,1024,4,48]{2,4,3,1,0:T(8,128)} %get-tuple-element.207, s32[]{:T(128)S(6)} %copy.89, f32[4,1024,1024]{1,2,0:T(8,128)S(1)} %get-tuple-element.187, f32[4,1024]{1,0:T(4,128)S(1)} %get-tuple-element.188, pred[1024]{0:T(1024)(128)(4,1)S(1)} %add_compare_fusion.4, ...), kind=kOutput, calls=%fused_computation.9.clone.1 | convolution fusion | flops 419430400 | bytes 17974280 | tf_op jit(solution)/shard_map/while/body/eval_jaxpr/shqk,skhd->sqhd/dot_general | solution.py:48
  117.9 4.1 %fusion.71 = f32[4,1024]{1,0:T(4,128)S(1)} fusion(f32[4,1024,1024]{1,2,0:T(8,128)S(1)} %get-tuple-element.187, f32[4,1024]{1,0:T(4,128)S(1)} %get-tuple-element.188, pred[1024]{0:T(1024)(128)(4,1)S(1)} %add_compare_fusion.4), kind=kLoop, calls=%fused_computation.5.clone.1 | loop fusion | flops 16773120 | bytes 16811008 | tf_op jit(solution)/shard_map/while/body/eval_jaxpr/reduce_sum | solution.py:47
  122.0 5.6 %fusion.72 = f32[4,1,1024,4,48]{2,4,3,1,0:T(8,128)} fusion(f32[4,1,1024,4,48]{2,4,3,1,0:T(8,128)} %get-tuple-element.207, s32[]{:T(128)S(6)} %copy.89, f32[4,1024,1024]{1,2,0:T(8,128)S(1)} %get-tuple-element.187, f32[4,1024]{1,0:T(4,128)S(1)} %get-tuple-element.188, pred[1024]{0:T(1024)(128)(4,1)S(1)} %add_compare_fusion.4, ...), kind=kOutput, calls=%fused_computation.9.clone.1 | convolution fusion | flops 419430400 | bytes 17974280 | tf_op jit(solution)/shard_map/while/body/eval_jaxpr/shqk,skhd->sqhd/dot_general | solution.py:48
  130.8 16.1 %all_gather.3 = bf16[512,768]{1,0:T(8,128)(2,1)S(1)} all-gather(bf16[64,768]{1,0:T(8,128)(2,1)S(1)} %reshape.260), channel_id=1, replica_groups=mesh['dp'=4,'seq'=8] {'seq'}, dimensions={0}, use_global_device_ids=true | all-gather | bytes 884736 | tf_op jit(solution)/shard_map/all_gather | solution.py:109
  154.2 3.9 %broadcast_in_dim.156 = f32[64,16,16,48]{3,2,1,0:T(8,128)} broadcast(f32[64,16,48]{2,1,0:T(8,128)S(1)} %copy.51), dimensions={0,2,3} | broadcast | bytes 3342336 | tf_op jit(solution)/shard_map/jit(_where)/broadcast_in_dim | solution.py:74
  158.1 6.6 %copy.53 = f32[1024,16,48]{0,2,1:T(8,128)} copy(f32[1024,16,48]{2,1,0:T(8,128)} %bitcast.163) | data formatting | bytes 6291456 | tf_op jit(solution)/shard_map/jit(_where)/broadcast_in_dim | solution.py:74
  164.7 4.0 %fusion.32 = bf16[1024,16,48]{0,2,1:T(8,128)(2,1)S(1)} fusion(f32[1024,16,48]{0,2,1:T(8,128)} %copy.53, f32[4,1,1024,4,48]{2,4,3,1,0:T(8,128)} %get-tuple-element.52, f32[1024,16]{0,1:T(8,128)S(1)} %get-tuple-element.111, f32[1024,16]{0,1:T(8,128)S(1)} %get-tuple-element.113, f32[1024,16]{0,1:T(8,128)S(1)} %get-tuple-element.112, ...), kind=kLoop, calls=%fused_computation.37 | loop fusion | flops 5505024 | bytes 8078336 | tf_op jit(solution)/shard_map/convert_element_type | solution.py:84
  175.1 7.7 %broadcast_in_dim.157 = f32[1024,768]{1,0:T(8,128)} reshape(f32[64,16,16,48]{3,2,1,0:T(8,128)} %broadcast_in_dim.156) | data formatting | bytes 6291456 | tf_op jit(solution)/shard_map/jit(_where)/broadcast_in_dim | solution.py:74
  182.8 3.6 %copy.52 = f32[1024,768]{0,1:T(8,128)} copy(f32[1024,768]{1,0:T(8,128)} %broadcast_in_dim.157) | data formatting | bytes 6291456 | tf_op jit(solution)/shard_map/jit(_where)/broadcast_in_dim | solution.py:74
  186.4 3.8 %fusion.31 = bf16[1024,768]{0,1:T(8,128)(2,1)S(1)} fusion(f32[1024,768]{0,1:T(8,128)} %copy.52, f32[4,1,1024,4,48]{2,4,3,1,0:T(8,128)} %get-tuple-element.52, f32[1024,16]{0,1:T(8,128)S(1)} %get-tuple-element.111, f32[1024,16]{0,1:T(8,128)S(1)} %get-tuple-element.113, f32[1024,16]{0,1:T(8,128)S(1)} %get-tuple-element.112, ...), kind=kLoop, calls=%fused_computation.36 | loop fusion | flops 5505024 | bytes 8078336 | tf_op jit(solution)/shard_map/convert_element_type | solution.py:84
  190.2 23.4 %reduce-scatter.4.cloned.1.call-done = f32[96,768]{1,0:T(8,128)} async-done(((f32[768,768]{1,0:T(8,128)}), f32[96,768]{1,0:T(8,128)}) %reduce-scatter.4.cloned.1.call-update) | async-done | bytes 294928
  215.4 4.0 %fusion.40 = bf16[1,1024,768]{2,1,0:T(8,128)(2,1)} fusion(bf16[1024,768]{0,1:T(8,128)(2,1)S(1)} %fusion.31, bf16[768,768]{1,0:T(8,128)(2,1)} %param.16), kind=kOutput, calls=%fused_computation.53 | convolution fusion | flops 1208745984 | bytes 4325376 | tf_op jit(solution)/shard_map/dot_general | solution.py:129
  219.4 39.2 %all-reduce.2.cloned.1.call-done = bf16[768,96]{1,0:T(8,128)(2,1)} async-done(((bf16[768,96]{1,0:T(8,128)(2,1)}), bf16[768,96]{1,0:T(8,128)(2,1)}) %all-reduce.2.cloned.1.call-update) | async-done | bytes 147472 | tf_op jit(solution)/shard_map/psum | solution.py:137
  (83 shorter events, 57.2 us)
Async XLA Ops:
  7.2 1.5 copy-start
  8.6 2.8 %copy-start.9 = (bf16[768,768]{1,0:T(8,128)(2,1)S(1)}, bf16[768,768]{1,0:T(8,128)(2,1)}, u32[]{:S(2)}) copy-start(bf16[768,768]{1,0:T(8,128)(2,1)} %param.14) | copy-start | bytes 3538948
  11.5 2.6 copy-start.10
  16.7 2.7 %copy-start.2 = (bf16[1024,768]{0,1:T(8,128)(2,1)S(1)}, bf16[1024,768]{0,1:T(8,128)(2,1)}, u32[]{:S(2)}) copy-start(bf16[1024,768]{0,1:T(8,128)(2,1)} %convolution_convert_fusion.2) | copy-start | bytes 4718596
  55.3 92.7 %all-to-all-start = ((bf16[8,64,768]{2,1,0:T(8,128)(2,1)}), bf16[8,64,768]{2,1,0:T(8,128)(2,1)}, u32[]{:S(2)}, u32[]{:S(2)}) async-start(bf16[8,64,768]{2,1,0:T(8,128)(2,1)} %stack.3), calls=%async_computation | async-start | bytes 1572864 | tf_op jit(solution)/shard_map/all_to_all | solution.py:104
  61.6 152.0 %reduce-scatter.4.cloned.1.call-start = ((), (), s32[]{:S(2)}) async-start(), calls=%async_computation.3 | async-start | bytes 2654208
  61.7 67.2 %copy-start.6 = (pred[16,16]{0,1:T(8,128)(4,1)S(1)}, pred[16,16]{0,1:T(8,128)(4,1)}, u32[]{:S(2)}) copy-start(pred[16,16]{0,1:T(8,128)(4,1)} %get-tuple-element.118) | copy-start | bytes 772
  128.2 19.0 %copy-start.3 = (f32[4,1,4,1024]{3,2,1,0:T(4,128)S(1)}, f32[4,1,4,1024]{3,2,1,0:T(4,128)}, u32[]{:S(2)}) copy-start(f32[4,1,4,1024]{3,2,1,0:T(4,128)} %get-tuple-element.53) | copy-start | bytes 196612
  128.2 19.6 %copy-start.7 = (s32[16]{0:T(128)S(1)}, s32[16]{0:T(128)}, u32[]{:S(2)}) copy-start(s32[16]{0:T(128)} %param.12) | copy-start | bytes 196
  158.1 6.6 %copy-start.4 = (pred[1024]{0:T(1024)(128)(4,1)S(1)}, pred[1024]{0:T(1024)(128)(4,1)}, u32[]{:S(2)}) copy-start(pred[1024]{0:T(1024)(128)(4,1)} %add_compare_fusion.2) | copy-start | bytes 3076
  164.7 4.0 %copy-start.8 = (bf16[1,1024,768]{2,1,0:T(8,128)(2,1)S(1)}, bf16[1,1024,768]{2,1,0:T(8,128)(2,1)}, u32[]{:S(2)}) copy-start(bf16[1,1024,768]{2,1,0:T(8,128)(2,1)} %param.17) | copy-start | bytes 4718596
  174.8 83.8 %all-reduce.2.cloned.1.call-start = ((), (), s32[]{:S(2)}) async-start(), calls=%async_computation.2 | async-start | bytes 393216 | tf_op jit(solution)/shard_map/psum | solution.py:137
  182.8 3.6 %copy-start.5 = (pred[1024]{0:T(1024)(128)(4,1)S(1)}, pred[1024]{0:T(1024)(128)(4,1)}, u32[]{:S(2)}) copy-start(pred[1024]{0:T(1024)(128)(4,1)} %add_compare_fusion.2) | copy-start | bytes 3076
  215.4 44.9 %copy-start.1 = (bf16[1,1024,768]{2,1,0:T(8,128)(2,1)S(1)}, bf16[1,1024,768]{2,1,0:T(8,128)(2,1)}, u32[]{:S(2)}) copy-start(bf16[1,1024,768]{2,1,0:T(8,128)(2,1)} %param.10) | copy-start | bytes 4718596
Sparse Core Ops, SparseCore 0:
  174.9 38.6 reduce-scatter.3
  217.1 41.4 all-reduce.1
